TPU v7x, 32 devices: a whole 2x2x4 slice. The times are simulated.
32 devices in a mesh: rep: 8 (over z, x), batch: 4 (over y, core).
Axes of the slice: x: 2, y: 2, z: 4, core: 2. Of those that a mesh axis runs over, the one named last changes fastest.
Arguments:
- embed: bfloat16 [4096, 1024], P(('rep', 'batch')), may hold values from -9 to 9
- actions: int32 [4096, 5], P(('rep', 'batch')), may hold values from 0 to 17
- rewards: float32 [4096, 5], P(('rep', 'batch')), may hold values from -1 to 1
- ends: int32 [4096, 5], P(('rep', 'batch')), may hold values 0 or 1
- behaviour: float32 [4096, 5, 18], P(('rep', 'batch')), may hold values from -5 to 5
- w_hidden: bfloat16 [1024, 1024], replicated, may hold values from -0.1875 to 0.1875
- w_action: bfloat16 [18, 1024], replicated, may hold values from -3 to 3
- w_heads: bfloat16 [1024, 36], replicated, may hold values from -0.1875 to 0.1875
Outputs:
- grad_hidden: float32 [1024, 1024], replicated
- grad_action: float32 [18, 1024], replicated
- grad_heads: float32 [1024, 36], replicated
- targets: float32 [4096, 5], P(('rep', 'batch'))
All inputs are finite; a program needn't handle non-finite values. No bound on the sum of `ends` on one device may be relied on, other than what follows from the above.
Results may differ from a plain program's by a relative error of at most 0.0057.
Values sent between devices are 32-bit elements; how exact they have to be, the bound alone decides.
A program may use at most 64 MiB of HBM per device.

v0:
```python
import jax
import jax.numpy as jnp
from jax import lax
from jax.sharding import PartitionSpec as P

DISCOUNT = 0.997
TRACE_LAMBDA = 0.95
EPSILON = 1e-06


def unroll(emb_block, act_block, w_hidden, w_action, w_heads):
    act_count = w_action.shape[0]
    unroll_len = act_block.shape[1]
    onehot = (
        act_block[:, :, None] == jnp.arange(act_count, dtype=jnp.int32)[None, None, :]
    ).astype(jnp.bfloat16)
    hidden_state = emb_block.astype(jnp.float32)
    rounded = []
    squashed = []
    head_out = []
    for step in range(unroll_len):
        state_bf16 = hidden_state.astype(jnp.bfloat16)
        rounded.append(state_bf16)
        head_out.append(jnp.dot(state_bf16, w_heads, preferred_element_type=jnp.float32))
        preact = jnp.dot(state_bf16, w_hidden, preferred_element_type=jnp.float32)
        preact = preact + jnp.dot(onehot[:, step], w_action, preferred_element_type=jnp.float32)
        squash = jnp.tanh(preact)
        squashed.append(squash)
        hidden_state = hidden_state + squash
    state_bf16 = hidden_state.astype(jnp.bfloat16)
    head_out.append(jnp.dot(state_bf16, w_heads, preferred_element_type=jnp.float32))
    return (jnp.stack(head_out), rounded, squashed, onehot)


def estimates(head_out, actions, rewards, ends, behaviour):
    act_count = behaviour.shape[-1]
    unroll_len = actions.shape[1]
    logits = head_out[:, :, :act_count]
    qvalues = head_out[:, :, act_count:]
    exp_logits = jnp.exp(logits)
    policy = exp_logits / jnp.sum(exp_logits, axis=-1, keepdims=True)
    values = jnp.sum(policy * qvalues, axis=-1)
    onehot_f = (
        jnp.transpose(actions)[:, :, None] == jnp.arange(act_count, dtype=jnp.int32)[None, None, :]
    ).astype(jnp.float32)
    logpol = logits[:unroll_len] - jnp.log(jnp.sum(exp_logits[:unroll_len], axis=-1, keepdims=True))
    behave = jnp.transpose(behaviour, (1, 0, 2))
    behave_log = behave - jnp.log(jnp.sum(jnp.exp(behave), axis=-1, keepdims=True))
    ratios = jnp.exp(jnp.sum(onehot_f * (logpol - behave_log), axis=-1))
    clipped = jnp.minimum(1.0, ratios)
    not_ended = 1.0 - jnp.transpose(ends).astype(jnp.float32)
    td_error = jnp.transpose(rewards) + DISCOUNT * not_ended * values[1:] - values[:unroll_len]
    carried = jnp.zeros_like(values[0])
    collected = []
    for step in range(unroll_len - 1, -1, -1):
        carried = (
            clipped[step] * td_error[step]
            + DISCOUNT * TRACE_LAMBDA * not_ended[step] * clipped[step] * carried
        )
        collected.append(carried)
    collected = jnp.stack(collected[::-1])
    targets = values[:unroll_len] + collected
    advantage = qvalues[:unroll_len] - values[:unroll_len, :, None]
    return (policy[:unroll_len], onehot_f, targets, advantage)


def objective(head_out, onehot_f, targets, cmpo_policy, taken_weight, norm_scale):
    act_count = onehot_f.shape[-1]
    unroll_len = onehot_f.shape[0]
    logits = head_out[:unroll_len, :, :act_count]
    qvalues = head_out[:unroll_len, :, act_count:]
    logpol = logits - jnp.log(jnp.sum(jnp.exp(logits), axis=-1, keepdims=True))
    q_taken = jnp.sum(onehot_f * qvalues, axis=-1)
    value_term = 0.5 * (q_taken - targets) ** 2
    policy_term = -taken_weight * jnp.sum(onehot_f * logpol, axis=-1)
    regular = -jnp.sum(cmpo_policy * logpol, axis=-1)
    return jnp.sum(value_term + policy_term + regular) * norm_scale


def backward(cotangent, rounded, squashed, onehot, w_hidden, w_heads):
    unroll_len = len(squashed)
    hid = w_hidden.shape[0]
    grad_state = jnp.zeros(squashed[0].shape, jnp.float32)
    grad_hidden = jnp.zeros((hid, hid), jnp.float32)
    grad_action = jnp.zeros((hid, onehot.shape[-1]), jnp.float32)
    grad_heads = jnp.zeros(w_heads.shape, jnp.float32)
    for step in range(unroll_len - 1, -1, -1):
        grad_pre = (grad_state * (1.0 - squashed[step] * squashed[step])).astype(jnp.bfloat16)
        head_cot = cotangent[step].astype(jnp.bfloat16)
        grad_hidden = grad_hidden + jnp.dot(
            rounded[step].T, grad_pre, preferred_element_type=jnp.float32
        )
        grad_action = grad_action + jnp.dot(
            grad_pre.T, onehot[:, step], preferred_element_type=jnp.float32
        )
        grad_heads = grad_heads + jnp.dot(
            rounded[step].T, head_cot, preferred_element_type=jnp.float32
        )
        grad_state = grad_state + jnp.dot(grad_pre, w_hidden.T, preferred_element_type=jnp.float32)
        grad_state = grad_state + jnp.dot(head_cot, w_heads.T, preferred_element_type=jnp.float32)
    return (grad_hidden, grad_action, grad_heads)


def body(embed, actions, rewards, ends, behaviour, w_hidden, w_action, w_heads):
    rows_here = embed.shape[0]
    unroll_len = actions.shape[1]
    act_count = w_action.shape[0]
    groups = lax.axis_size("batch")
    devices = lax.axis_size("rep") * groups
    head_out, rounded, squashed, onehot = unroll(embed, actions, w_hidden, w_action, w_heads)
    policy, onehot_f, targets, advantage = estimates(head_out, actions, rewards, ends, behaviour)
    spread = lax.psum(jnp.sum(advantage * advantage), "batch")
    spread_scale = jnp.sqrt(spread / (groups * rows_here * unroll_len * act_count) + EPSILON)
    weights = jnp.exp(jnp.clip(advantage / spread_scale, -1.0, 1.0))
    norm_mass = jnp.sum(policy * weights, axis=-1)
    mass_sum = lax.psum(jnp.sum(norm_mass), "batch")
    mean_mass = mass_sum / (groups * rows_here * unroll_len)
    cmpo_policy = policy * weights / norm_mass[:, :, None]
    taken_weight = jnp.sum(onehot_f * weights, axis=-1) / mean_mass
    cotangent = jax.grad(objective)(
        head_out,
        onehot_f,
        targets,
        cmpo_policy,
        taken_weight,
        1.0 / (devices * rows_here * unroll_len),
    )
    grad_hidden, grad_action, grad_heads = backward(
        cotangent, rounded, squashed, onehot, w_hidden, w_heads
    )
    grad_hidden, grad_action, grad_heads = lax.psum(
        (grad_hidden, grad_action, grad_heads), ("rep", "batch")
    )
    return (grad_hidden, grad_action.T, grad_heads, targets.T)


def solution(mesh):
    placed = (
        P(("rep", "batch"), None),
        P(("rep", "batch"), None),
        P(("rep", "batch"), None),
        P(("rep", "batch"), None),
        P(("rep", "batch"), None, None),
        P(),
        P(),
        P(),
    )
    return jax.shard_map(
        body,
        mesh=mesh,
        in_specs=placed,
        out_specs=(P(), P(), P(), P(("rep", "batch"), None)),
        check_vma=False,
    )
```

profile of v0, /device:TPU:0, one launch (start us, length us, event | category | flops | bytes accessed | tf_op | source)
XLA Modules:
  0.0 216.6 jit_solution(16951233208367975323)
XLA Ops:
  7.2 0.9 iota_compare_fusion.1
  8.1 0.7 copy-done
  8.8 1.4 fusion.52
  11.7 1.1 fusion.48
  13.6 0.4 fusion.56
  14.3 0.8 fusion.41
  15.1 1.6 fusion.45
  16.7 2.7 %fusion.46 = f32[1024,1024]{1,0:T(8,128)} fusion(bf16[128,1024]{1,0:T(8,128)(2,1)S(1)} %get-tuple-element.46, f32[128,1024]{1,0:T(8,128)S(1)} %fusion.4), kind=kOutput, calls=%fused_computation.125 | convolution fusion | flops 268959744 | bytes 4980736 | tf_op jit(solution)/shard_map/dot_general | solution.py:90
  21.0 0.7 slice_exponential_fusion
  21.6 0.6 multiply_reduce_fusion
  22.3 9.0 %psum.35 = f32[]{:T(128)} all-reduce(f32[]{:T(128)} %multiply_reduce_fusion), channel_id=1, replica_groups=mesh['rep'=8,'batch'=4] {'batch'}, use_global_device_ids=true, to_apply=%region_7.8 | all-reduce | flops 1 | bytes 8 | tf_op jit(solution)/shard_map/psum | solution.py:112
  32.1 2.2 %select_reduce_fusion.1 = (f32[5,128]{1,0:T(8,128)S(1)}, f32[5,128]{1,0:T(8,128)}, f32[5,128]{1,0:T(8,128)}, f32[]{:T(128)}, f32[5,128,18]{1,2,0:T(8,128)}) fusion(f32[5,128,36]{1,2,0:T(8,128)} %copy-done.14, s32[5,128]{1,0:T(8,128)S(1)} %bitcast.143, f32[]{:T(128)S(6)} %sqrt.3, f32[5,128]{1,0:T(8,128)S(1)} %get-tuple-element.40, ...), kind=kLoop, calls=%fused_computation.71 | loop fusion | flops 124799 | bytes 197128 | tf_op jit(solution)/shard_map/jvp()/reduce_sum | solution.py:73
  34.2 6.4 %psum.36 = f32[]{:T(128)} all-reduce(f32[]{:T(128)} %get-tuple-element.25), channel_id=1, replica_groups=mesh['rep'=8,'batch'=4] {'batch'}, use_global_device_ids=true, to_apply=%region_11.12 | all-reduce | flops 1 | bytes 8 | tf_op jit(solution)/shard_map/psum | solution.py:116
  40.7 0.6 add_bitcast_fusion
  42.1 0.8 negate_multiply_fusion
  42.8 0.9 fusion.50
  43.8 0.7 negate_divide_fusion
  44.5 0.9 multiply_add_fusion
  45.3 1.1 fusion.60
  47.0 0.8 fusion.10
  48.1 0.7 fusion.57
  48.9 0.8 convolution_add_fusion.6
  50.2 0.7 fusion.58
  50.9 0.8 convolution_add_fusion.5
  52.2 0.7 fusion.59
  53.0 0.8 convolution_add_fusion.4
  54.6 0.8 fusion.11
  55.4 3.1 %bitcast_add_fusion = f32[1024,1024]{1,0:T(8,128)} fusion(f32[1024,1024]{1,0:T(8,128)S(1)} %fusion.59, f32[1024,1024]{1,0:T(8,128)S(1)} %fusion.58, f32[1024,1024]{1,0:T(8,128)S(1)} %copy-done.1, f32[1024,1024]{1,0:T(8,128)S(1)} %fusion.57, bf16[128,1024]{1,0:T(8,128)(2,1)S(1)} %fusion.9, bf16[128,1024]{1,0:T(8,128)(2,1)S(1)} %copy-done.2), kind=kOutput, calls=%fused_computation.3 | convolution fusion | flops 272629760 | bytes 21495808 | tf_op jit(solution)/shard_map/dot_general | solution.py:90
  58.4 145.2 %all-reduce.5.cloned.1.call-done = (f32[1024,1024]{1,0:T(8,128)}, f32[18,1024]{1,0:T(8,128)}, f32[1024,36]{0,1:T(8,128)}) async-done(((f32[1024,1024]{1,0:T(8,128)}, f32[18,1024]{1,0:T(8,128)}, f32[1024,36]{0,1:T(8,128)}), (f32[1024,1024]{1,0:T(8,128)}, f32[18,1024]{1,0:T(8,128)}, f32[1024,36]{0,1:T(8,128)})) %all-reduce.5.cloned.1.call-update) | async-done | bytes 4415504 | tf_op jit(solution)/shard_map/psum | solution.py:131
  203.6 4.8 %copy.28 = f32[1024,1024]{1,0:T(8,128)} copy(f32[1024,1024]{1,0:T(8,128)} %get-tuple-element.57) | data formatting | bytes 8388608
  208.4 0.6 copy.29
  209.1 0.7 copy.30
  (81 shorter events, 6.5 us)
Async XLA Ops:
  7.2 1.6 copy-start
  7.2 3.0 %copy-start.2 = (bf16[128,1024]{1,0:T(8,128)(2,1)S(1)}, bf16[128,1024]{1,0:T(8,128)(2,1)}, u32[]{:S(2)}) copy-start(bf16[128,1024]{1,0:T(8,128)(2,1)} %param.8) | copy-start | bytes 786436
  7.2 3.0 %copy-start.13 = (bf16[18,1024]{1,0:T(8,128)(2,1)S(1)}, bf16[18,1024]{1,0:T(8,128)(2,1)}, u32[]{:S(2)}) copy-start(bf16[18,1024]{1,0:T(8,128)(2,1)} %param.14) | copy-start | bytes 110596
  7.2 196.4 %all-reduce.5.cloned.1.call-start = ((), (), s32[]{:S(2)}) async-start(), calls=%async_computation | async-start | bytes 8912896 | tf_op jit(solution)/shard_map/psum | solution.py:131
  8.8 5.5 %copy-start.17 = (pred[128,5,18]{0,2,1:T(8,128)(4,1)}, pred[128,5,18]{0,2,1:T(8,128)(4,1)S(1)}, u32[]{:S(2)}) copy-start(pred[128,5,18]{0,2,1:T(8,128)(4,1)S(1)} %iota_compare_fusion.1) | copy-start | bytes 34564
  10.5 9.4 %copy-start.4 = (bf16[128,1024]{1,0:T(8,128)(2,1)}, bf16[128,1024]{1,0:T(8,128)(2,1)S(1)}, u32[]{:S(2)}) copy-start(bf16[128,1024]{1,0:T(8,128)(2,1)S(1)} %get-tuple-element.41) | copy-start | bytes 786436
  11.2 1.5 copy-start.7
  13.5 7.0 %copy-start.6 = (bf16[128,1024]{1,0:T(8,128)(2,1)}, bf16[128,1024]{1,0:T(8,128)(2,1)S(1)}, u32[]{:S(2)}) copy-start(bf16[128,1024]{1,0:T(8,128)(2,1)S(1)} %get-tuple-element.46) | copy-start | bytes 786436
  13.5 7.2 %copy-start.9 = (f32[128,1024]{1,0:T(8,128)}, f32[128,1024]{1,0:T(8,128)S(1)}, u32[]{:S(2)}) copy-start(f32[128,1024]{1,0:T(8,128)S(1)} %get-tuple-element.47) | copy-start | bytes 1572868
  16.7 2.8 %copy-start.22 = (s32[128,5]{0,1:T(8,128)S(1)}, s32[128,5]{0,1:T(8,128)}, u32[]{:S(2)}) copy-start(s32[128,5]{0,1:T(8,128)} %param.11) | copy-start | bytes 7684
  16.7 2.8 %copy-start.21 = (f32[128,5,18]{0,2,1:T(8,128)S(1)}, f32[128,5,18]{0,2,1:T(8,128)}, u32[]{:S(2)}) copy-start(f32[128,5,18]{0,2,1:T(8,128)} %param.12) | copy-start | bytes 138244
  16.7 2.9 %copy-start.3 = (bf16[1024,36]{0,1:T(8,128)(2,1)S(1)}, bf16[1024,36]{0,1:T(8,128)(2,1)}, u32[]{:S(2)}) copy-start(bf16[1024,36]{0,1:T(8,128)(2,1)} %param.15) | copy-start | bytes 221188
  19.5 2.1 copy-start.23
  19.5 2.8 %copy-start.20 = (s32[128,5]{0,1:T(8,128)S(1)}, s32[128,5]{0,1:T(8,128)}, u32[]{:S(2)}) copy-start(s32[128,5]{0,1:T(8,128)} %param.9) | copy-start | bytes 7684
  20.7 1.6 copy-start.14
  42.0 4.8 %copy-start.5 = (bf16[128,1024]{1,0:T(8,128)(2,1)S(1)}, bf16[128,1024]{1,0:T(8,128)(2,1)}, u32[]{:S(2)}) copy-start(bf16[128,1024]{1,0:T(8,128)(2,1)} %copy-done.4) | copy-start | bytes 786436
  42.0 5.8 %copy-start.10 = (f32[128,1024]{1,0:T(8,128)S(1)}, f32[128,1024]{1,0:T(8,128)}, u32[]{:S(2)}) copy-start(f32[128,1024]{1,0:T(8,128)} %copy-done.9) | copy-start | bytes 1572868
  42.0 5.8 %copy-start.12 = (f32[128,1024]{1,0:T(8,128)S(1)}, f32[128,1024]{1,0:T(8,128)}, u32[]{:S(2)}) copy-start(f32[128,1024]{1,0:T(8,128)} %fusion.45) | copy-start | bytes 1572868
  48.8 1.0 copy-start.11
  50.9 1.0 copy-start.8
  52.9 1.1 copy-start.15
  52.9 1.1 copy-start.18
  52.9 2.4 %copy-start.1 = (f32[1024,1024]{1,0:T(8,128)S(1)}, f32[1024,1024]{1,0:T(8,128)}, u32[]{:S(2)}) copy-start(f32[1024,1024]{1,0:T(8,128)} %fusion.46) | copy-start | bytes 12582916
  203.6 4.8 %copy-start.19 = (f32[18,1024]{1,0:T(8,128)S(1)}, f32[18,1024]{1,0:T(8,128)}, u32[]{:S(2)}) copy-start(f32[18,1024]{1,0:T(8,128)} %get-tuple-element.58) | copy-start | bytes 221188
  203.6 5.5 %copy-start.16 = (f32[1024,36]{0,1:T(8,128)S(1)}, f32[1024,36]{0,1:T(8,128)}, u32[]{:S(2)}) copy-start(f32[1024,36]{0,1:T(8,128)} %get-tuple-element.59) | copy-start | bytes 442372
Sparse Core Ops, SparseCore 0:
  58.6 145.0 all-reduce.4
where the time goes:
time: 217 us
  waiting for transfers between devices  145 us (67%)
  matrix products  24.2 us (11%)
  between operations  15.9 us (7%)
  blocking collectives  15.5 us (7%)
  other arithmetic  8.42 us (4%)
  local copies, waits for them, and re-layouts  7.38 us (3%)
    psum x1, waiting for transfers between devices, body(): lax.psum((grad_hidden, grad_action, grad_heads), ('rep', 'batch'))  145 us
    psum x1, blocking collectives, body(): spread = lax.psum(jnp.sum(advantage * advantage), 'batch')  9.04 us
    dot_general x5, matrix products, backward(): jnp.dot(rounded[step].T, grad_pre, preferred_element_type=jnp.float32)  7.97 us
    unnamed x51, local copies, waits for them, and re-layouts  7.36 us
    psum x1, blocking collectives, body(): mass_sum = lax.psum(jnp.sum(norm_mass), 'batch')  6.44 us
  transfers between devices with their start and end apart: 1, of which 1 were waited for; matrix products, arithmetic and copies ran while one was open for 0% of the time, Pallas kernels for 0%

commit v1 on v0

v1 whole, which is shorter than its diff:
```python
import functools

import jax
import jax.numpy as jnp
from jax import lax
from jax.experimental import pallas as pl
from jax.experimental.pallas import tpu as pltpu
from jax.sharding import PartitionSpec as P

DISCOUNT = 0.997
TRACE_LAMBDA = 0.95
EPSILON = 1e-06
MESH = pl.DeviceIdType.MESH
COLORS = 4
F32 = jnp.float32
BF16 = jnp.bfloat16


def place_of(device):
    coords = getattr(device, "coords", None)
    if coords is None:
        return None
    return tuple(coords) + (getattr(device, "core_on_chip", 0),)


def topology(mesh):
    devices = mesh.devices
    origin = place_of(devices[(0,) * devices.ndim])
    dims = {}
    for position, axis in enumerate(mesh.axis_names):
        stride = 1
        while stride < devices.shape[position]:
            index = [0] * devices.ndim
            index[position] = stride
            here = place_of(devices[tuple(index)])
            if here is None or origin is None:
                last = position == devices.ndim - 1 and stride == 1
                key, far = ((3,) if last else (0, position, stride)), 1
            else:
                moved = [d for d in range(len(here)) if here[d] != origin[d]]
                key, far = (moved[0],), abs(here[moved[0]] - origin[moved[0]])
            dims.setdefault(key, []).append((far, (axis, stride)))
            stride *= 2
    core = dims.pop((3,))[0][1]
    chips = [[bit for _, bit in sorted(dims[key])] for key in sorted(dims)]
    return core, chips


def color_orders(chips):
    near = [bits[0] for bits in chips]
    rest = [bit for bits in chips for bit in bits[1:]]
    if len(near) == 3:
        perms = ((0, 1, 2), (1, 0, 2), (2, 0, 1), (1, 2, 0))
    else:
        n = len(near)
        perms = [[(i + j) % n for j in range(n)] for i in range(COLORS)]
    return [[near[i] for i in perm] + rest for perm in perms]


def subsets(bits):
    out = [()]
    for bit in bits:
        out = out + [s + (bit,) for s in out]
    return [s for s in out if s]


def bit_value(bit):
    axis, stride = bit
    return lax.rem(lax.axis_index(axis) // stride, 2)


def partner(bits):
    where = {}
    for axis, stride in bits:
        at = lax.axis_index(axis)
        moved = where.get(axis, at)
        where[axis] = moved + (1 - 2 * lax.rem(at // stride, 2)) * stride
    return where


def dot(a, b, ca, cb):
    return lax.dot_general(a, b, (((ca,), (cb,)), ((), ())), preferred_element_type=F32)


def main_kernel(
    cfg, embed_in, act_in, rew_in, ends_in, beh_in, wh_in, wa_in, wht_in,
    out, tgt, embed, act, rew, ends, beh, wh, wa, wht, in_sem,
    grads, rcore, rbuf, s_all, x_all, s_t, deriv, h_ref, r_ref, whp32, whp, wap, onehot, g32, g_all,
    ssend, srecv,
    ss_sem, sr_sem, c1s, c1r, rss, rsr, ags, agr, c2s, c2r,
):
    core_bit, orders, group, everyone, devices, group_count = cfg
    rows, hid = embed.shape
    steps = act.shape[0]
    acts = wa.shape[0]
    apad = wap.shape[0]
    qrow = whp.shape[0] // 2
    total_rows = grads.shape[1]
    width = grads.shape[2]
    stages = len(orders[0])

    loads = []
    for i, (source, target) in enumerate((
        (embed_in, embed), (act_in, act), (rew_in, rew), (ends_in, ends),
        (beh_in, beh), (wa_in, wa), (wht_in, wht), (wh_in, wh),
    )):
        loads.append(pltpu.make_async_copy(source, target, in_sem.at[i]))
        loads[-1].start()

    barrier = pltpu.get_barrier_semaphore()
    for bits in everyone:
        pl.semaphore_signal(barrier, inc=1, device_id=partner(bits), device_id_type=MESH)

    for load in loads[:-1]:
        load.wait()

    whp32[...] = jnp.zeros_like(whp32)
    whp32[0:acts, :] = wht[0:acts, :].astype(F32)
    whp32[qrow : qrow + acts, :] = wht[acts : 2 * acts, :].astype(F32)
    whp[...] = whp32[...].astype(BF16)
    whp32[...] = jnp.zeros_like(whp32)
    whp32[0:acts, :] = wa[...].astype(F32)
    wap[...] = whp32[0:apad, :].astype(BF16)
    rows_iota = lax.broadcasted_iota(jnp.int32, (apad, rows), 0)
    for k in range(steps):
        hot = rows_iota == act[k : k + 1, :]
        onehot[:, k * rows : (k + 1) * rows] = jnp.where(hot, 1.0, 0.0).astype(BF16)

    loads[-1].wait()
    heads = []
    h_ref[...] = embed[...].astype(F32)
    for k in range(steps + 1):
        s = h_ref[...].astype(BF16)
        if k < steps:
            s_all[k * rows : (k + 1) * rows, :] = s
            pre = dot(s, wh[...], 1, 0) + dot(onehot[:, k * rows : (k + 1) * rows], wap[...], 0, 0)
            t = jnp.tanh(pre)
            h_ref[...] = h_ref[...] + t
            if k < steps - 1:
                deriv[k] = 1.0 - t * t
                s_t[:, k * rows : (k + 1) * rows] = s.T
        heads.append(dot(whp[...], s, 1, 1))

    logits = [o[0:acts] for o in heads]
    qs = [o[qrow : qrow + acts] for o in heads]
    pis, values, logpis, hots, clipped = [], [], [], [], []
    small_iota = lax.broadcasted_iota(jnp.int32, (acts, rows), 0)
    for k in range(steps + 1):
        e = jnp.exp(logits[k])
        z = jnp.sum(e, axis=0, keepdims=True)
        pi = e / z
        pis.append(pi)
        values.append(jnp.sum(pi * qs[k], axis=0, keepdims=True))
        if k < steps:
            logpi = logits[k] - jnp.log(z)
            b = beh[k]
            mu = b - jnp.log(jnp.sum(jnp.exp(b), axis=0, keepdims=True))
            hot = jnp.where(small_iota == act[k : k + 1, :], 1.0, 0.0)
            hots.append(hot)
            ratio = jnp.exp(jnp.sum(hot * (logpi - mu), axis=0, keepdims=True))
            clipped.append(jnp.minimum(1.0, ratio))
    carried = jnp.zeros_like(values[0])
    targets = [None] * steps
    for k in range(steps - 1, -1, -1):
        live = 1.0 - ends[k : k + 1, :].astype(F32)
        delta = rew[k : k + 1, :] + DISCOUNT * live * values[k + 1] - values[k]
        carried = clipped[k] * delta + DISCOUNT * TRACE_LAMBDA * live * clipped[k] * carried
        targets[k] = values[k] + carried
        tgt[k : k + 1, :] = targets[k]
    advs = [qs[k] - values[k] for k in range(steps)]

    pl.semaphore_wait(barrier, len(everyone))

    def group_sum(slot, value):
        ssend[slot] = jnp.broadcast_to(value, ssend.shape[1:])
        copies = [
            pltpu.make_async_remote_copy(
                src_ref=ssend.at[slot], dst_ref=srecv.at[slot, i],
                send_sem=ss_sem.at[slot, i], recv_sem=sr_sem.at[slot, i],
                device_id=partner(bits), device_id_type=MESH,
            )
            for i, bits in enumerate(group)
        ]
        for copy in copies:
            copy.start()

        def finish():
            for copy in copies:
                copy.wait()
            total = ssend[slot]
            for i in range(len(group)):
                total = total + srecv[slot, i]
            return total[0:1, 0:1]

        return finish

    def total_of(parts):
        acc = parts[0]
        for part in parts[1:]:
            acc = acc + part
        return jnp.sum(jnp.sum(acc, axis=0, keepdims=True), axis=1, keepdims=True)

    spread = group_sum(0, total_of([a * a for a in advs]))()
    sigma = jnp.sqrt(spread / (group_count * rows * steps * acts) + EPSILON)
    weights = [jnp.exp(jnp.clip(a / sigma, -1.0, 1.0)) for a in advs]
    mass = [jnp.sum(pis[k] * weights[k], axis=0, keepdims=True) for k in range(steps)]
    finish = group_sum(1, total_of(mass))
    scale = 1.0 / (devices * rows * steps)
    g32[...] = jnp.zeros_like(g32)
    partial = []
    for k in range(steps):
        cmpo = pis[k] * weights[k] / mass[k]
        partial.append(pis[k] * jnp.sum(cmpo, axis=0, keepdims=True) - cmpo)
        taken_q = jnp.sum(hots[k] * qs[k], axis=0, keepdims=True)
        g32[k, qrow : qrow + acts, :] = hots[k] * ((taken_q - targets[k]) * scale)
    mean_mass = finish() / (group_count * rows * steps)
    for k in range(steps):
        taken_w = jnp.sum(hots[k] * weights[k], axis=0, keepdims=True) / mean_mass
        g32[k, 0:acts, :] = (partial[k] + taken_w * (pis[k] - hots[k])) * scale
        g_all[:, k * rows : (k + 1) * rows] = g32[k].astype(BF16)

    def head_part(k):
        return dot(g_all[:, k * rows : (k + 1) * rows], whp[...], 0, 0)

    r_ref[...] = head_part(steps - 1)
    for k in range(steps - 2, -1, -1):
        x = (r_ref[...] * deriv[k]).astype(BF16)
        x_all[k * rows : (k + 1) * rows, :] = x
        if k > 0:
            r_ref[...] = r_ref[...] + head_part(k)
            x = x_all[k * rows : (k + 1) * rows, :]
            for at in range(0, hid, 2 * width):
                cols = slice(at, at + 2 * width)
                r_ref[:, cols] = r_ref[:, cols] + dot(wh[cols, :], x, 1, 1).T

    core = bit_value(core_bit)
    other = 1 - core
    used = apad // 8 * 8
    heads_at = hid + used
    ends_at = heads_at + 2 * qrow

    def gradient(owner, color):
        at = pl.multiple_of((owner * COLORS + color) * width, width)
        xb = x_all[:, pl.ds(at, 2 * width)]
        sb = s_all[:, pl.ds(at, 2 * width)]
        gh = dot(s_t[...], xb, 1, 0)
        ga = dot(onehot[:, 0 : (steps - 1) * rows], xb, 1, 0)
        gd = dot(g_all[...], sb, 1, 0)
        for i in range(2):
            slot = owner * COLORS + color + i
            cols = slice(i * width, (i + 1) * width)
            grads[slot, 0:hid, :] = gh[:, cols]
            grads[slot, hid:heads_at, :] = ga[:, cols]
            grads[slot, heads_at:ends_at, :] = gd[:, cols]
            if ends_at < total_rows:
                grads[slot, ends_at:, :] = jnp.zeros((total_rows - ends_at, width), F32)

    mate = partner((core_bit,))
    to_core = []
    for pair in range(0, COLORS, 2):
        gradient(other, pair)
        for color in (pair, pair + 1):
            copy = pltpu.make_async_remote_copy(
                src_ref=grads.at[other * COLORS + color], dst_ref=rcore.at[color],
                send_sem=c1s.at[color], recv_sem=c1r.at[color],
                device_id=mate, device_id_type=MESH,
            )
            copy.start()
            to_core.append(copy)
    for pair in range(0, COLORS, 2):
        gradient(core, pair)

    low = [0] * COLORS
    kept = [[] for _ in range(COLORS)]
    flying = [[] for _ in range(COLORS)]

    def add(color, row, source, src_row, count, target):
        mine = core * COLORS + color
        row = pl.multiple_of(row, 8)
        src_row = pl.multiple_of(src_row, 8)
        target[mine, pl.ds(row, count), :] = (
            grads[mine, pl.ds(row, count), :] + source[color, pl.ds(src_row, count), :]
        )

    offset = 0
    length = total_rows
    for stage in range(stages):
        half = length // 2
        for color in range(COLORS):
            mine = core * COLORS + color
            if stage == 0:
                to_core[color].wait_recv()
                source, base = rcore, 0
            else:
                flying[color][-1].wait_recv()
                source, base = rbuf, offset - length
            v = bit_value(orders[color][stage])
            send, keep = (1 - v) * half, v * half
            add(color, low[color] + send, source, base + send, half, grads)
            copy = pltpu.make_async_remote_copy(
                src_ref=grads.at[mine, pl.ds(pl.multiple_of(low[color] + send, 8), half)],
                dst_ref=rbuf.at[color, pl.ds(offset, half)],
                send_sem=rss.at[color, stage], recv_sem=rsr.at[color, stage],
                device_id=partner((orders[color][stage],)), device_id_type=MESH,
            )
            copy.start()
            flying[color].append(copy)
            add(color, low[color] + keep, source, base + keep, half, grads)
            low[color] = low[color] + keep
            kept[color].append(keep)
        offset += half
        length = half

    to_mate = [[] for _ in range(COLORS)]
    doubling = [[] for _ in range(COLORS)]

    def forward(color, row, count):
        mine = core * COLORS + color
        piece = out.at[mine, pl.ds(pl.multiple_of(row, 8), count)]
        i = len(to_mate[color])
        copy = pltpu.make_async_remote_copy(
            src_ref=piece, dst_ref=piece,
            send_sem=c2s.at[color, i], recv_sem=c2r.at[color, i],
            device_id=mate, device_id_type=MESH,
        )
        copy.start()
        to_mate[color].append(copy)

    def double(color, stage, row, count):
        mine = core * COLORS + color
        piece = out.at[mine, pl.ds(pl.multiple_of(row, 8), count)]
        copy = pltpu.make_async_remote_copy(
            src_ref=piece, dst_ref=piece,
            send_sem=ags.at[color, stage], recv_sem=agr.at[color, stage],
            device_id=partner((orders[color][stage],)), device_id_type=MESH,
        )
        copy.start()
        doubling[color].append(copy)

    for color in range(COLORS):
        flying[color][-1].wait_recv()
        add(color, low[color], rbuf, offset - length, length, out)
        double(color, stages - 1, low[color], length)
        forward(color, low[color], length)
    for stage in range(stages - 1, -1, -1):
        for color in range(COLORS):
            doubling[color][-1].wait_recv()
            keep = kept[color][stage]
            start = low[color] - keep
            if stage > 0:
                double(color, stage - 1, start, 2 * length)
            forward(color, start + length - keep, length)
            low[color] = start
        length *= 2
    for color in range(COLORS):
        for copy in to_mate[color]:
            copy.wait_recv()
    for color in range(COLORS):
        to_core[color].wait_send()
        for copy in flying[color] + doubling[color] + to_mate[color]:
            copy.wait_send()


def layout_kernel(apad, qrow, packed, tgt_in, gh, ga, gd, tgt, sems):
    groups, _, width = packed.shape
    hid = gh.shape[0]
    acts = ga.shape[0]
    copies = []
    for i in range(groups):
        copy = pltpu.make_async_copy(
            packed.at[i, pl.ds(0, hid)], gh.at[:, pl.ds(i * width, width)], sems.at[i]
        )
        copy.start()
        copies.append(copy)
    tgt[...] = tgt_in[...]
    first = hid + apad
    for i in range(groups):
        cols = slice(i * width, (i + 1) * width)
        ga[:, cols] = packed[i, hid : hid + acts, :]
        gd[0:acts, cols] = packed[i, first : first + acts, :]
        gd[acts : 2 * acts, cols] = packed[i, first + qrow : first + qrow + acts, :]
    for copy in copies:
        copy.wait()


def body(plan, embed, actions, rewards, ends, behaviour, w_hidden, w_action, w_heads):
    core_bit, chips, group = plan
    rows, hid = embed.shape
    steps = actions.shape[1]
    acts = w_action.shape[0]
    group_count = lax.axis_size("batch")
    devices = lax.axis_size("rep") * group_count
    orders = color_orders(chips)
    stages = len(orders[0])
    everyone = list(group)
    for bit in [core_bit] + orders[0]:
        if (bit,) not in everyone:
            everyone.append((bit,))
    apad = -(-acts // 16) * 16
    qrow = -(-acts // 32) * 32
    unit = 8 << stages
    total_rows = -(-(hid + apad + 2 * qrow) // unit) * unit
    groups = 2 * COLORS
    width = hid // groups
    cfg = (core_bit, orders, group, everyone, devices, group_count)
    vmem = pl.BlockSpec(memory_space=pltpu.VMEM)
    dma = pltpu.SemaphoreType.DMA
    packed, tgt = pl.pallas_call(
        functools.partial(main_kernel, cfg),
        out_shape=(
            pltpu.VMEM((groups, total_rows, width), F32),
            jax.ShapeDtypeStruct((steps, rows), F32),
        ),
        in_specs=[pl.BlockSpec(memory_space=pltpu.HBM)] * 8,
        out_specs=(vmem, vmem),
        scratch_shapes=[
            pltpu.VMEM((rows, hid), BF16),
            pltpu.VMEM((steps, rows), jnp.int32),
            pltpu.VMEM((steps, rows), F32),
            pltpu.VMEM((steps, rows), jnp.int32),
            pltpu.VMEM((steps, acts, rows), F32),
            pltpu.VMEM((hid, hid), BF16),
            pltpu.VMEM((acts, hid), BF16),
            pltpu.VMEM((2 * acts, hid), BF16),
            dma((8,)),
            pltpu.VMEM((groups, total_rows, width), F32),
            pltpu.VMEM((COLORS, total_rows, width), F32),
            pltpu.VMEM((COLORS, total_rows, width), F32),
            pltpu.VMEM((steps * rows, hid), BF16),
            pltpu.VMEM(((steps - 1) * rows, hid), BF16),
            pltpu.VMEM((hid, (steps - 1) * rows), BF16),
            pltpu.VMEM((steps - 1, rows, hid), F32),
            pltpu.VMEM((rows, hid), F32),
            pltpu.VMEM((rows, hid), F32),
            pltpu.VMEM((2 * qrow, hid), F32),
            pltpu.VMEM((2 * qrow, hid), BF16),
            pltpu.VMEM((apad, hid), BF16),
            pltpu.VMEM((apad, steps * rows), BF16),
            pltpu.VMEM((steps, 2 * qrow, rows), F32),
            pltpu.VMEM((2 * qrow, steps * rows), BF16),
            pltpu.VMEM((2, 8, 128), F32),
            pltpu.VMEM((2, len(group), 8, 128), F32),
            dma((2, len(group))),
            dma((2, len(group))),
            dma((COLORS,)),
            dma((COLORS,)),
            dma((COLORS, stages)),
            dma((COLORS, stages)),
            dma((COLORS, stages)),
            dma((COLORS, stages)),
            dma((COLORS, stages + 1)),
            dma((COLORS, stages + 1)),
        ],
        compiler_params=pltpu.CompilerParams(
            collective_id=0, has_side_effects=True, vmem_limit_bytes=48 * 1024 * 1024
        ),
    )(
        embed, actions.T, rewards.T, ends.T, jnp.transpose(behaviour, (1, 2, 0)),
        w_hidden, w_action, w_heads.T,
    )
    gh, ga, gd, tgt = pl.pallas_call(
        functools.partial(layout_kernel, apad, qrow),
        out_shape=(
            jax.ShapeDtypeStruct((hid, hid), F32),
            jax.ShapeDtypeStruct((acts, hid), F32),
            jax.ShapeDtypeStruct((2 * acts, hid), F32),
            jax.ShapeDtypeStruct((steps, rows), F32),
        ),
        in_specs=[vmem, vmem],
        out_specs=(pl.BlockSpec(memory_space=pl.ANY), vmem, vmem, vmem),
        scratch_shapes=[dma((groups,))],
        compiler_params=pltpu.CompilerParams(vmem_limit_bytes=16 * 1024 * 1024),
    )(packed, tgt)
    return gh, ga, gd.T, tgt.T


def solution(mesh):
    core_bit, chips = topology(mesh)
    batch_bits = []
    stride = 1
    while stride < mesh.shape["batch"]:
        batch_bits.append(("batch", stride))
        stride *= 2
    plan = (core_bit, chips, subsets(batch_bits))
    rows = P(("rep", "batch"), None)
    placed = (rows, rows, rows, rows, P(("rep", "batch"), None, None), P(), P(), P())
    return jax.shard_map(
        functools.partial(body, plan),
        mesh=mesh,
        in_specs=placed,
        out_specs=(P(), P(), P(), rows),
        check_vma=False,
    )
```

time: 217 us -> 86.7 us (0.40)
  waiting for transfers between devices: 145 us -> 0 us
  Pallas kernels: 0 us -> 80.1 us
  matrix products: 24.2 us -> 0 us
  blocking collectives: 15.5 us -> 0 us
  between operations: 15.9 us -> 0.66 us
  other arithmetic: 8.42 us -> 0 us
    psum x1 -> x0, waiting for transfers between devices: 145 us -> none  [body(): lax.psum((grad_hidden, grad_action, grad_heads), ('rep', 'batch'))]
    pallas_call x0 -> x2, Pallas kernels: none -> 80.1 us  [the longest x1 77.3 us: body(): pl.pallas_call(functools.partial(main_kernel, cfg), out_shape=(pltpu.VMEM...]
    dot_general x39 -> x0, matrix products: 24.2 us -> none  [the longest x5 7.97 us: backward(): jnp.dot(rounded[step].T, grad_pre, preferred_element_type=jnp.float32)]
    psum x2 -> x0, blocking collectives: 15.5 us -> none  [the longest x1 9.04 us: body(): spread = lax.psum(jnp.sum(advantage * advantage), 'batch')]
    reduce_sum x4 -> x0, other arithmetic: 2.99 us -> none  [the longest x1 2.18 us: objective(): q_taken = jnp.sum(onehot_f * qvalues, axis=-1)]
    div x3 -> x0, other arithmetic: 2.29 us -> none  [the longest x1 0.94 us: body(): cmpo_policy = policy * weights / norm_mass[:, :, None]]
    unnamed x51 -> x14, local copies, waits for them, and re-layouts: 7.36 us -> 5.51 us
  transfers between devices with their start and end apart: 1 -> 0, of which waited for: 1 -> 0; matrix products, arithmetic and copies ran while one was open for 0% -> 0% of each run, Pallas kernels for 0% -> 0%
where the time goes in v1:
time: 86.7 us; the launch traced here: 86.3 us
  Pallas kernels  80.1 us (92%)
  local copies, waits for them, and re-layouts  5.51 us (6%)
    pallas_call x1, Pallas kernels, body(): pl.pallas_call(functools.partial(main_kernel, cfg), out_shape=(pltpu.VMEM...  77.3 us
    unnamed x14, local copies, waits for them, and re-layouts  5.51 us
    pallas_call x1, Pallas kernels, body(): pl.pallas_call(functools.partial(layout_kernel, apad, qrow), out_shape=(j...  2.77 us

profile of v1, /device:TPU:0, one launch (start us, length us, event | category | flops | bytes accessed | tf_op | source)
XLA Modules:
  0.0 86.3 jit_solution(9694712202177412153)
XLA Ops:
  0.6 0.0 copy-start
  0.6 0.9 %copy-done = bf16[128,1024]{1,0:T(8,128)(2,1)S(1)} copy-done((bf16[128,1024]{1,0:T(8,128)(2,1)S(1)}, bf16[128,1024]{1,0:T(8,128)(2,1)}, u32[]{:S(2)}) %copy-start) | copy-done | bytes 262168
  1.6 0.0 copy-start.1
  1.6 0.9 %copy-done.1 = bf16[1024,36]{0,1:T(8,128)(2,1)S(1)} copy-done((bf16[1024,36]{0,1:T(8,128)(2,1)S(1)}, bf16[1024,36]{0,1:T(8,128)(2,1)}, u32[]{:S(2)}) %copy-start.1) | copy-done | bytes 73752
  2.5 0.0 copy-start.2
  2.5 0.8 copy-done.2
  3.3 0.0 copy-start.3
  3.3 0.8 copy-done.3
  4.1 0.0 copy-start.4
  4.1 0.7 copy-done.4
  4.8 0.0 copy-start.5
  4.8 0.7 copy-done.5
  5.5 0.0 copy-start.6
  5.5 0.7 copy-done.6
  6.2 77.3 %shard_map.111 = (f32[8,1152,128]{2,1,0:T(8,128)S(1)}, f32[5,128]{1,0:T(8,128)S(1)}) custom-call(bf16[128,1024]{1,0:T(8,128)(2,1)S(1)} %copy-done, s32[5,128]{1,0:T(8,128)S(1)} %bitcast.9, f32[5,128]{1,0:T(8,128)S(1)} %bitcast.10, s32[5,128]{1,0:T(8,128)S(1)} %bitcast.11, f32[5,18,128]{2,1,0:T(8,128)S(1)} %bitcast.8, bf16[1024,1024]{1,0:T(8,128)(2,1)} %wh_in.1, ...), custom_call_target="tpu_custom_call" | custom-call | tf_op jit(solution)/shard_map/pallas_call | solution.py:408
  83.5 2.8 %shard_map.112 = (f32[1024,1024]{1,0:T(8,128)}, f32[18,1024]{1,0:T(8,128)}, f32[36,1024]{1,0:T(8,128)}, f32[5,128]{1,0:T(8,128)}) custom-call(f32[8,1152,128]{2,1,0:T(8,128)S(1)} %get-tuple-element.10.packed, f32[5,128]{1,0:T(8,128)S(1)} %get-tuple-element.11.tgt_in), custom_call_target="tpu_custom_call" | custom-call | tf_op jit(solution)/shard_map/pallas_call | solution.py:461
Async XLA Ops:
  0.6 1.0 %copy-start = (bf16[128,1024]{1,0:T(8,128)(2,1)S(1)}, bf16[128,1024]{1,0:T(8,128)(2,1)}, u32[]{:S(2)}) copy-start(bf16[128,1024]{1,0:T(8,128)(2,1)} %embed_in.1) | copy-start | bytes 786436
  1.6 0.9 %copy-start.1 = (bf16[1024,36]{0,1:T(8,128)(2,1)S(1)}, bf16[1024,36]{0,1:T(8,128)(2,1)}, u32[]{:S(2)}) copy-start(bf16[1024,36]{0,1:T(8,128)(2,1)} %param.15) | copy-start | bytes 221188
  2.5 0.8 copy-start.2
  3.3 0.8 copy-start.3
  4.1 0.7 copy-start.4
  4.8 0.7 copy-start.5
  5.5 0.7 copy-start.6

commit v2 on v1

--- a/solution.py
+++ b/solution.py
@@ -12,6 +12,7 @@
 EPSILON = 1e-06
 MESH = pl.DeviceIdType.MESH
 COLORS = 4
+PARTS = 3
 F32 = jnp.float32
 BF16 = jnp.bfloat16
 
@@ -50,10 +51,11 @@
     near = [bits[0] for bits in chips]
     rest = [bit for bits in chips for bit in bits[1:]]
     if len(near) == 3:
-        perms = ((0, 1, 2), (1, 0, 2), (2, 0, 1), (1, 2, 0))
+        turns = ((0, 1, 2), (1, 2, 0), (2, 0, 1))
+        perms = [turns[i % PARTS] for i in range(COLORS * PARTS)]
     else:
         n = len(near)
-        perms = [[(i + j) % n for j in range(n)] for i in range(COLORS)]
+        perms = [[(i + j) % n for j in range(n)] for i in range(COLORS * PARTS)]
     return [[near[i] for i in perm] + rest for perm in perms]
 
 
@@ -270,11 +272,15 @@
     for pair in range(0, COLORS, 2):
         gradient(core, pair)
 
-    low = [0] * COLORS
-    kept = [[] for _ in range(COLORS)]
-    flying = [[] for _ in range(COLORS)]
-
-    def add(color, row, source, src_row, count, target):
+    chains = COLORS * PARTS
+    part = total_rows // PARTS
+    first = [(c % PARTS) * part for c in range(chains)]
+    low = list(first)
+    kept = [[] for _ in range(chains)]
+    flying = [[] for _ in range(chains)]
+
+    def add(chain, row, source, src_row, count, target):
+        color = chain // PARTS
         mine = core * COLORS + color
         row = pl.multiple_of(row, 8)
         src_row = pl.multiple_of(src_row, 8)
@@ -283,81 +289,84 @@
         )
 
     offset = 0
-    length = total_rows
+    length = part
     for stage in range(stages):
         half = length // 2
-        for color in range(COLORS):
+        for chain in range(chains):
+            color = chain // PARTS
             mine = core * COLORS + color
             if stage == 0:
-                to_core[color].wait_recv()
-                source, base = rcore, 0
+                if chain % PARTS == 0:
+                    to_core[color].wait_recv()
+                source, base = rcore, first[chain]
             else:
-                flying[color][-1].wait_recv()
-                source, base = rbuf, offset - length
-            v = bit_value(orders[color][stage])
+                flying[chain][-1].wait_recv()
+                source, base = rbuf, first[chain] + offset - length
+            v = bit_value(orders[chain][stage])
             send, keep = (1 - v) * half, v * half
-            add(color, low[color] + send, source, base + send, half, grads)
+            add(chain, low[chain] + send, source, base + send, half, grads)
             copy = pltpu.make_async_remote_copy(
-                src_ref=grads.at[mine, pl.ds(pl.multiple_of(low[color] + send, 8), half)],
-                dst_ref=rbuf.at[color, pl.ds(offset, half)],
-                send_sem=rss.at[color, stage], recv_sem=rsr.at[color, stage],
-                device_id=partner((orders[color][stage],)), device_id_type=MESH,
+                src_ref=grads.at[mine, pl.ds(pl.multiple_of(low[chain] + send, 8), half)],
+                dst_ref=rbuf.at[color, pl.ds(first[chain] + offset, half)],
+                send_sem=rss.at[chain, stage], recv_sem=rsr.at[chain, stage],
+                device_id=partner((orders[chain][stage],)), device_id_type=MESH,
             )
             copy.start()
-            flying[color].append(copy)
-            add(color, low[color] + keep, source, base + keep, half, grads)
-            low[color] = low[color] + keep
-            kept[color].append(keep)
+            flying[chain].append(copy)
+            add(chain, low[chain] + keep, source, base + keep, half, grads)
+            low[chain] = low[chain] + keep
+            kept[chain].append(keep)
         offset += half
         length = half
 
-    to_mate = [[] for _ in range(COLORS)]
-    doubling = [[] for _ in range(COLORS)]
-
-    def forward(color, row, count):
-        mine = core * COLORS + color
+    to_mate = [[] for _ in range(chains)]
+    doubling = [[] for _ in range(chains)]
+
+    def forward(chain, row, count):
+        mine = core * COLORS + chain // PARTS
         piece = out.at[mine, pl.ds(pl.multiple_of(row, 8), count)]
-        i = len(to_mate[color])
+        i = len(to_mate[chain])
         copy = pltpu.make_async_remote_copy(
             src_ref=piece, dst_ref=piece,
-            send_sem=c2s.at[color, i], recv_sem=c2r.at[color, i],
+            send_sem=c2s.at[chain, i], recv_sem=c2r.at[chain, i],
             device_id=mate, device_id_type=MESH,
         )
         copy.start()
-        to_mate[color].append(copy)
-
-    def double(color, stage, row, count):
-        mine = core * COLORS + color
+        to_mate[chain].append(copy)
+
+    def double(chain, stage, row, count):
+        mine = core * COLORS + chain // PARTS
         piece = out.at[mine, pl.ds(pl.multiple_of(row, 8), count)]
         copy = pltpu.make_async_remote_copy(
             src_ref=piece, dst_ref=piece,
-            send_sem=ags.at[color, stage], recv_sem=agr.at[color, stage],
-            device_id=partner((orders[color][stage],)), device_id_type=MESH,
+            send_sem=ags.at[chain, stage], recv_sem=agr.at[chain, stage],
+            device_id=partner((orders[chain][stage],)), device_id_type=MESH,
         )
         copy.start()
-        doubling[color].append(copy)
-
-    for color in range(COLORS):
-        flying[color][-1].wait_recv()
-        add(color, low[color], rbuf, offset - length, length, out)
-        double(color, stages - 1, low[color], length)
-        forward(color, low[color], length)
+        doubling[chain].append(copy)
+
+    for chain in range(chains):
+        flying[chain][-1].wait_recv()
+        add(chain, low[chain], rbuf, first[chain] + offset - length, length, out)
+        double(chain, stages - 1, low[chain], length)
+        forward(chain, low[chain], length)
     for stage in range(stages - 1, -1, -1):
-        for color in range(COLORS):
-            doubling[color][-1].wait_recv()
-            keep = kept[color][stage]
-            start = low[color] - keep
+        for chain in range(chains):
+            doubling[chain][-1].wait_recv()
+            keep = kept[chain][stage]
+            start = low[chain] - keep
             if stage > 0:
-                double(color, stage - 1, start, 2 * length)
-            forward(color, start + length - keep, length)
-            low[color] = start
+                double(chain, stage - 1, start, 2 * length)
+            forward(chain, start + length - keep, length)
+            low[chain] = start
         length *= 2
-    for color in range(COLORS):
-        for copy in to_mate[color]:
+    for chain in range(chains):
+        for copy in to_mate[chain]:
             copy.wait_recv()
     for color in range(COLORS):
         to_core[color].wait_send()
-        for copy in flying[color] + doubling[color] + to_mate[color]:
+    for chain in range(chains):
+        for copy in flying[chain] + doubling[chain] + to_mate[chain]:
             copy.wait_send()
 
 
@@ -398,7 +407,7 @@
             everyone.append((bit,))
     apad = -(-acts // 16) * 16
     qrow = -(-acts // 32) * 32
-    unit = 8 << stages
+    unit = PARTS * 8 << stages
     total_rows = -(-(hid + apad + 2 * qrow) // unit) * unit
     groups = 2 * COLORS
     width = hid // groups
@@ -444,12 +453,12 @@
             dma((2, len(group))),
             dma((COLORS,)),
             dma((COLORS,)),
-            dma((COLORS, stages)),
-            dma((COLORS, stages)),
-            dma((COLORS, stages)),
-            dma((COLORS, stages)),
-            dma((COLORS, stages + 1)),
-            dma((COLORS, stages + 1)),
+            dma((COLORS * PARTS, stages)),
+            dma((COLORS * PARTS, stages)),
+            dma((COLORS * PARTS, stages)),
+            dma((COLORS * PARTS, stages)),
+            dma((COLORS * PARTS, stages + 1)),
+            dma((COLORS * PARTS, stages + 1)),
         ],
         compiler_params=pltpu.CompilerParams(
             collective_id=0, has_side_effects=True, vmem_limit_bytes=48 * 1024 * 1024

time: 86.7 us -> 77.8 us (0.90)
  Pallas kernels: 80.1 us -> 71.1 us
    pallas_call x1, Pallas kernels: 77.3 us -> 68.3 us  [body(): pl.pallas_call(functools.partial(main_kernel, cfg), out_shape=(pltpu.VMEM...]
where the time goes in v2:
time: 77.8 us; the launch traced here: 77.3 us
  Pallas kernels  71.1 us (91%)
  local copies, waits for them, and re-layouts  5.51 us (7%)
    pallas_call x1, Pallas kernels, body(): pl.pallas_call(functools.partial(main_kernel, cfg), out_shape=(pltpu.VMEM...  68.3 us
    unnamed x14, local copies, waits for them, and re-layouts  5.51 us
    pallas_call x1, Pallas kernels, body(): pl.pallas_call(functools.partial(layout_kernel, apad, qrow), out_shape=(j...  2.77 us

profile of v2, /device:TPU:0, one launch (start us, length us, event | category | flops | bytes accessed | tf_op | source)
XLA Modules:
  0.0 77.3 jit_solution(18274665017284365246)
XLA Ops:
  0.6 0.0 copy-start
  0.6 0.9 %copy-done = bf16[128,1024]{1,0:T(8,128)(2,1)S(1)} copy-done((bf16[128,1024]{1,0:T(8,128)(2,1)S(1)}, bf16[128,1024]{1,0:T(8,128)(2,1)}, u32[]{:S(2)}) %copy-start) | copy-done | bytes 262168
  1.6 0.0 copy-start.1
  1.6 0.9 %copy-done.1 = bf16[1024,36]{0,1:T(8,128)(2,1)S(1)} copy-done((bf16[1024,36]{0,1:T(8,128)(2,1)S(1)}, bf16[1024,36]{0,1:T(8,128)(2,1)}, u32[]{:S(2)}) %copy-start.1) | copy-done | bytes 73752
  2.5 0.0 copy-start.2
  2.5 0.8 %copy-done.2 = f32[128,5,18]{0,2,1:T(8,128)S(1)} copy-done((f32[128,5,18]{0,2,1:T(8,128)S(1)}, f32[128,5,18]{0,2,1:T(8,128)}, u32[]{:S(2)}) %copy-start.2) | copy-done | bytes 46104
  3.3 0.0 copy-start.3
  3.3 0.8 %copy-done.3 = bf16[18,1024]{1,0:T(8,128)(2,1)S(1)} copy-done((bf16[18,1024]{1,0:T(8,128)(2,1)S(1)}, bf16[18,1024]{1,0:T(8,128)(2,1)}, u32[]{:S(2)}) %copy-start.3) | copy-done | bytes 36888
  4.1 0.0 copy-start.4
  4.1 0.7 copy-done.4
  4.8 0.0 copy-start.5
  4.8 0.7 copy-done.5
  5.5 0.0 copy-start.6
  5.5 0.7 copy-done.6
  6.2 68.3 %shard_map.111 = (f32[8,1152,128]{2,1,0:T(8,128)S(1)}, f32[5,128]{1,0:T(8,128)S(1)}) custom-call(bf16[128,1024]{1,0:T(8,128)(2,1)S(1)} %copy-done, s32[5,128]{1,0:T(8,128)S(1)} %bitcast.9, f32[5,128]{1,0:T(8,128)S(1)} %bitcast.10, s32[5,128]{1,0:T(8,128)S(1)} %bitcast.11, f32[5,18,128]{2,1,0:T(8,128)S(1)} %bitcast.8, bf16[1024,1024]{1,0:T(8,128)(2,1)} %wh_in.1, ...), custom_call_target="tpu_custom_call" | custom-call | tf_op jit(solution)/shard_map/pallas_call | solution.py:417
  74.5 2.8 %shard_map.112 = (f32[1024,1024]{1,0:T(8,128)}, f32[18,1024]{1,0:T(8,128)}, f32[36,1024]{1,0:T(8,128)}, f32[5,128]{1,0:T(8,128)}) custom-call(f32[8,1152,128]{2,1,0:T(8,128)S(1)} %get-tuple-element.10.packed, f32[5,128]{1,0:T(8,128)S(1)} %get-tuple-element.11.tgt_in), custom_call_target="tpu_custom_call" | custom-call | tf_op jit(solution)/shard_map/pallas_call | solution.py:470
Async XLA Ops:
  0.6 1.0 %copy-start = (bf16[128,1024]{1,0:T(8,128)(2,1)S(1)}, bf16[128,1024]{1,0:T(8,128)(2,1)}, u32[]{:S(2)}) copy-start(bf16[128,1024]{1,0:T(8,128)(2,1)} %embed_in.1) | copy-start | bytes 786436
  1.6 0.9 %copy-start.1 = (bf16[1024,36]{0,1:T(8,128)(2,1)S(1)}, bf16[1024,36]{0,1:T(8,128)(2,1)}, u32[]{:S(2)}) copy-start(bf16[1024,36]{0,1:T(8,128)(2,1)} %param.15) | copy-start | bytes 221188
  2.5 0.8 %copy-start.2 = (f32[128,5,18]{0,2,1:T(8,128)S(1)}, f32[128,5,18]{0,2,1:T(8,128)}, u32[]{:S(2)}) copy-start(f32[128,5,18]{0,2,1:T(8,128)} %param.12) | copy-start | bytes 138244
  3.3 0.8 %copy-start.3 = (bf16[18,1024]{1,0:T(8,128)(2,1)S(1)}, bf16[18,1024]{1,0:T(8,128)(2,1)}, u32[]{:S(2)}) copy-start(bf16[18,1024]{1,0:T(8,128)(2,1)} %wa_in.1) | copy-start | bytes 110596
  4.1 0.7 copy-start.4
  4.8 0.7 copy-start.5
  5.5 0.7 copy-start.6
